TPU v7x, 512 devices: a whole 4x4x16 slice. The times are simulated.
512 devices in a mesh: gx: 64 (over y, z), ta: 8 (over x, core).
Axes of the slice: x: 4, y: 4, z: 16, core: 2. Of those that a mesh axis runs over, the one named last changes fastest.
Arguments:
- query_vecs: bfloat16 [256, 64, 5120], P('gx', None, 'ta'), may hold values from -32 to 32
- key_vecs: bfloat16 [256, 64, 5120], P('gx', None, 'ta'), may hold values from -6 to 6
- value_vecs: bfloat16 [256, 64, 5120], P('gx', None, 'ta'), may hold values from -6 to 6
- slot_map: int32 [16, 64], replicated, may hold values from 0 to 63, each once within a row
- edge_list: int32 [256, 2], replicated, may hold values from 0 to 63
- edge_types: int32 [256], replicated, may hold values from 0 to 2
- type_gain: float32 [2, 3, 5120], P(None, None, 'ta'), may hold values from 0.25 to 2
- norm_gain: float32 [2, 5120], P(None, 'ta'), may hold values from 0.5 to 2
- gate_proj: bfloat16 [2, 5120, 20480], P(None, 'ta', 'gx'), may hold values from -0.078125 to 0.078125
- up_proj: bfloat16 [2, 5120, 20480], P(None, 'ta', 'gx'), may hold values from -0.078125 to 0.078125
- down_proj: bfloat16 [2, 20480, 5120], P(None, 'gx', 'ta'), may hold values from -0.0390625 to 0.0390625
Outputs:
- node_states: bfloat16 [512, 5120], P('gx', 'ta')
All inputs are finite; a program needn't handle non-finite values.
Results may differ from a plain program's by a relative error of at most 0.04.
Values may be sent and summed in bfloat16 or wider, within the bound.
A program may use at most 64 MiB of HBM per device.

v0:
```python
import jax
import jax.numpy as jnp
from jax import lax
from jax.sharding import PartitionSpec as P

D = 5120
HEAD_DIM = 128
VENUES = 16
STEPS = 16
NODE_STEPS = 8
ROUNDS = 2
ETYPES = 3


def settle_rows(nodes, hidden, down_local, row_begin, rows_dev):
    summed = lax.psum_scatter(
        jnp.dot(hidden, down_local, preferred_element_type=jnp.float32),
        "gx",
        scatter_dimension=0,
        tiled=True,
    )
    base_rows = lax.dynamic_slice_in_dim(nodes, row_begin, rows_dev, 0)
    return (base_rows.astype(jnp.float32) + summed).astype(jnp.bfloat16)


def per_device(
    query_vecs,
    key_vecs,
    value_vecs,
    slot_map,
    edge_list,
    edge_types,
    type_gain,
    norm_gain,
    gate_proj,
    up_proj,
    down_proj,
):
    pairs_dev = query_vecs.shape[0]
    inst_total = query_vecs.shape[1]
    feat_width = query_vecs.shape[2]
    head_count = feat_width // HEAD_DIM
    gx_count = lax.axis_size("gx")
    inst_local = inst_total // gx_count
    score_scale = 1.0 / HEAD_DIM**0.5
    venue_idx = lax.axis_index("gx") * pairs_dev // STEPS
    slot_order = lax.dynamic_index_in_dim(slot_map, venue_idx, 0, keepdims=False)
    split_shape = (pairs_dev, gx_count, inst_local, feat_width)
    sorted_queries = jnp.take(query_vecs, slot_order, axis=1).reshape(split_shape)
    sorted_keys = jnp.take(key_vecs, slot_order, axis=1).reshape(split_shape)
    sorted_values = jnp.take(value_vecs, slot_order, axis=1).reshape(split_shape)
    query_steps = jnp.arange(VENUES * NODE_STEPS) % NODE_STEPS + (STEPS - NODE_STEPS)
    key_steps = jnp.arange(VENUES * STEPS) % STEPS
    allowed = key_steps[None, :] <= query_steps[:, None]
    queries = lax.all_to_all(sorted_queries, "gx", split_axis=1, concat_axis=0, tiled=True)
    keyset = lax.all_to_all(sorted_keys, "gx", split_axis=1, concat_axis=0, tiled=True)
    valueset = lax.all_to_all(sorted_values, "gx", split_axis=1, concat_axis=0, tiled=True)
    pair_total = queries.shape[0]
    item_count = queries.shape[2]
    queries = queries.reshape(VENUES, STEPS, item_count, head_count, HEAD_DIM)[
        :, STEPS - NODE_STEPS :
    ]
    queries = queries.reshape(VENUES * NODE_STEPS, item_count, head_count, HEAD_DIM)
    keyset = keyset.reshape(pair_total, item_count, head_count, HEAD_DIM)
    valueset = valueset.reshape(pair_total, item_count, head_count, HEAD_DIM)
    scores = (
        jnp.einsum("qnhd,knhd->nhqk", queries, keyset, preferred_element_type=jnp.float32)
        * score_scale
    )
    scores = jnp.where(allowed[None, None], scores, jnp.float32(-1e30))
    row_max = jnp.max(scores, axis=-1, keepdims=True)
    expd = jnp.exp(scores - row_max)
    probs = (expd / jnp.sum(expd, axis=-1, keepdims=True)).astype(jnp.bfloat16)
    attended = jnp.einsum("nhqk,knhd->nqhd", probs, valueset, preferred_element_type=jnp.float32)
    attended = attended.reshape(item_count, VENUES, NODE_STEPS, feat_width)
    pooled = jnp.mean(attended, axis=1).astype(jnp.bfloat16)
    own_rows = pooled.reshape(inst_local * NODE_STEPS, feat_width)
    rows_dev = own_rows.shape[0]
    row_begin = lax.axis_index("gx") * rows_dev
    nodes = lax.all_gather(own_rows, "gx", axis=0, tiled=True)
    row_total = nodes.shape[0]
    node_ids = jnp.arange(inst_total)
    type_ids = jnp.arange(ETYPES)
    at_source = (edge_list[:, 0][:, None] == node_ids[None, :]).astype(jnp.float32)
    at_target = (edge_list[:, 1][:, None] == node_ids[None, :]).astype(jnp.float32)
    of_type = (edge_types[:, None] == type_ids[None, :]).astype(jnp.float32)
    adjacency = jnp.einsum("et,ei,ej->tij", of_type, at_target, at_source)
    degree = jnp.maximum(jnp.sum(at_target, axis=0), 1.0)
    adj_rows = adjacency.reshape(ETYPES * inst_total, inst_total).astype(jnp.bfloat16)
    for layer_idx in range(ROUNDS):
        flat_nodes = nodes.reshape(inst_total, NODE_STEPS * feat_width)
        gathered = jnp.dot(adj_rows, flat_nodes, preferred_element_type=jnp.float32)
        gathered = gathered.reshape(ETYPES, inst_total, NODE_STEPS, feat_width)
        message = (
            jnp.sum(gathered * type_gain[layer_idx][:, None, None, :], axis=0)
            / degree[:, None, None]
        )
        pre_norm = nodes.astype(jnp.float32) + message.reshape(row_total, feat_width)
        squares = lax.psum(jnp.sum(pre_norm * pre_norm, axis=-1), "ta")
        row_scale = lax.rsqrt(squares / D + 1e-05)[:, None]
        normed = (pre_norm * row_scale * norm_gain[layer_idx][None, :]).astype(jnp.bfloat16)
        gate_part = jnp.dot(normed, gate_proj[layer_idx], preferred_element_type=jnp.float32)
        up_part = jnp.dot(normed, up_proj[layer_idx], preferred_element_type=jnp.float32)
        gate_sum, up_sum = (
            lax.psum(gate_part.astype(jnp.bfloat16), "ta").astype(jnp.float32),
            lax.psum(up_part.astype(jnp.bfloat16), "ta").astype(jnp.float32),
        )
        hidden = (jax.nn.silu(gate_sum) * up_sum).astype(jnp.bfloat16)
        down_local = down_proj[layer_idx]
        if layer_idx == ROUNDS - 1:
            own_rows = settle_rows(nodes, hidden, down_local, row_begin, rows_dev)
        else:
            own_rows = settle_rows(nodes, hidden, down_local, row_begin, rows_dev)
            nodes = lax.all_gather(own_rows, "gx", axis=0, tiled=True)
    return own_rows


def solution(mesh):
    placed = (
        P("gx", None, "ta"),
        P("gx", None, "ta"),
        P("gx", None, "ta"),
        P(),
        P(),
        P(),
        P(None, None, "ta"),
        P(None, "ta"),
        P(None, "ta", "gx"),
        P(None, "ta", "gx"),
        P(None, "gx", "ta"),
    )
    return jax.shard_map(
        per_device, mesh=mesh, in_specs=placed, out_specs=P("gx", "ta"), check_vma=False
    )
```

profile of v0, /device:TPU:2, one launch (start us, length us, event | category | flops | bytes accessed | tf_op | source)
XLA Modules:
  0.0 1049.3 jit_solution(5708310502350677954)
XLA Ops:
  6.5 0.7 compare_and_fusion
  7.3 0.2 copy-done
  7.5 1.6 gather_fusion
  9.1 1.6 gather_fusion.1
  10.8 1.6 gather_fusion.2
  12.4 0.2 select_bitcast_fusion.1
  12.5 1.0 copy.32
  13.5 18.9 %all-to-all-start.1 = ((bf16[4,64,1,640]{3,0,2,1:T(4,128)(2,1)}), bf16[4,64,1,640]{3,0,2,1:T(4,128)(2,1)S(1)}, u32[]{:S(2)}, u32[]{:S(2)}) async-start(bf16[4,64,1,640]{3,0,2,1:T(4,128)(2,1)} %copy.32), calls=%async_computation.1 | async-start | bytes 655360 | tf_op jit(solution)/shard_map/all_to_all | solution.py:55
  32.4 1.0 copy.34
  33.4 22.7 %all-to-all-done.1 = bf16[4,64,1,640]{3,0,2,1:T(4,128)(2,1)S(1)} async-done(((bf16[4,64,1,640]{3,0,2,1:T(4,128)(2,1)}), bf16[4,64,1,640]{3,0,2,1:T(4,128)(2,1)S(1)}, u32[]{:S(2)}, u32[]{:S(2)}) %all-to-all-start.1) | async-done | bytes 327712 | tf_op jit(solution)/shard_map/all_to_all | solution.py:55
  56.1 6.5 all-to-all-start.2
  62.6 1.0 copy.31
  63.6 0.1 fusion.49
  63.8 0.1 div.64
  64.0 21.6 %all-to-all-done.2 = bf16[4,64,1,640]{3,0,2,1:T(4,128)(2,1)S(1)} async-done(((bf16[4,64,1,640]{3,0,2,1:T(4,128)(2,1)}), bf16[4,64,1,640]{3,0,2,1:T(4,128)(2,1)S(1)}, u32[]{:S(2)}, u32[]{:S(2)}) %all-to-all-start.2) | async-done | bytes 327712 | tf_op jit(solution)/shard_map/all_to_all | solution.py:56
  85.6 6.6 all-to-all-start
  92.2 0.2 fusion.6
  92.5 0.1 reshape.143
  92.7 0.1 reshape.146
  92.9 0.5 fusion.68
  93.3 0.3 fusion.5
  93.6 20.9 %all-to-all-done = bf16[4,64,1,640]{3,0,2,1:T(4,128)(2,1)S(1)} async-done(((bf16[4,64,1,640]{3,0,2,1:T(4,128)(2,1)}), bf16[4,64,1,640]{3,0,2,1:T(4,128)(2,1)S(1)}, u32[]{:S(2)}, u32[]{:S(2)}) %all-to-all-start) | async-done | bytes 327712 | tf_op jit(solution)/shard_map/all_to_all | solution.py:57
  114.5 0.1 reshape.141
  114.6 1.4 convolution_bitcast_fusion
  116.0 0.2 copy.37
  116.4 99.8 %all_gather.6 = bf16[512,640]{1,0:T(8,128)(2,1)S(1)} all-gather(bf16[8,640]{1,0:T(8,128)(2,1)S(1)} %multiply_convert_fusion.2), channel_id=1, replica_groups=mesh['gx'=64,'ta'=8] {'gx'}, dimensions={0}, use_global_device_ids=true | all-gather | bytes 665600 | tf_op jit(solution)/shard_map/all_gather | solution.py:80
  216.2 0.3 reshape.148
  216.5 0.7 multiply_reduce_fusion.1
  217.2 0.9 multiply_reduce_fusion.3
  218.1 10.0 psum.42
  228.1 1.3 convolution_convert_fusion.3
  229.4 1.3 convolution_convert_fusion.2
  230.7 67.0 %all-reduce.15.cloned.1.call-done = (bf16[512,320]{0,1:T(8,128)(2,1)}, bf16[512,320]{0,1:T(8,128)(2,1)}) async-done(((bf16[512,320]{0,1:T(8,128)(2,1)}, bf16[512,320]{0,1:T(8,128)(2,1)}), (bf16[512,320]{0,1:T(8,128)(2,1)}, bf16[512,320]{0,1:T(8,128)(2,1)})) %all-reduce.15.cloned.1.call-update) | async-done | bytes 655376 | tf_op jit(solution)/shard_map/psum | solution.py:106
  297.7 2.9 fusion.23
  300.7 1.3 dynamic-slice
  302.6 275.2 %all-reduce.9.cloned.1.call-done = f32[512,640]{1,0:T(8,128)} async-done(((f32[512,640]{1,0:T(8,128)}), f32[512,640]{1,0:T(8,128)}) %all-reduce.9.cloned.1.call-update) | async-done | bytes 1310736
  577.8 0.7 fusion.51
  578.6 98.7 %all_gather.7 = bf16[512,640]{1,0:T(8,128)(2,1)S(1)} all-gather(bf16[8,640]{1,0:T(8,128)(2,1)S(1)} %fusion.51), channel_id=1, replica_groups=mesh['gx'=64,'ta'=8] {'gx'}, dimensions={0}, use_global_device_ids=true | all-gather | bytes 665600 | tf_op jit(solution)/shard_map/all_gather | solution.py:114
  677.3 0.3 reshape.149
  677.6 0.7 multiply_reduce_fusion
  678.3 0.9 multiply_reduce_fusion.2
  679.2 10.0 psum.45
  689.2 1.3 convolution_convert_fusion.1
  690.5 1.2 convolution_convert_fusion
  691.8 69.7 %all-reduce.13.cloned.1.call-done = (bf16[512,320]{0,1:T(8,128)(2,1)}, bf16[512,320]{0,1:T(8,128)(2,1)}) async-done(((bf16[512,320]{0,1:T(8,128)(2,1)}, bf16[512,320]{0,1:T(8,128)(2,1)}), (bf16[512,320]{0,1:T(8,128)(2,1)}, bf16[512,320]{0,1:T(8,128)(2,1)})) %all-reduce.13.cloned.1.call-update) | async-done | bytes 655376 | tf_op jit(solution)/shard_map/psum | solution.py:106
  761.5 2.8 fusion.19
  764.3 277.2 %all-reduce.11.cloned.1.call-done = f32[512,640]{1,0:T(8,128)} async-done(((f32[512,640]{1,0:T(8,128)}), f32[512,640]{1,0:T(8,128)}) %all-reduce.11.cloned.1.call-update) | async-done | bytes 1310736
  1041.4 1.3 fusion.50
  (48 shorter events, 0.7 us)
Async XLA Ops:
  6.5 1.0 copy-start
  7.5 1.6 copy-start.1
  9.1 1.6 copy-start.2
  13.5 50.0 %copy-start.6 = (f32[2,3,640]{2,0,1:T(2,128)S(1)}, f32[2,3,640]{2,0,1:T(2,128)}, u32[]{:S(2)}) copy-start(f32[2,3,640]{2,0,1:T(2,128)} %param.19) | copy-start | bytes 46084
  13.5 50.1 %copy-start.8 = (s32[256,2]{0,1:T(2,128)S(1)}, s32[256,2]{0,1:T(2,128)}, u32[]{:S(2)}) copy-start(s32[256,2]{0,1:T(2,128)} %param.17) | copy-start | bytes 6148
  13.5 50.4 %copy-start.7 = (f32[2,640]{1,0:T(2,128)S(1)}, f32[2,640]{1,0:T(2,128)}, u32[]{:S(2)}) copy-start(f32[2,640]{1,0:T(2,128)} %param.20) | copy-start | bytes 15364
  13.5 42.6 %all-to-all-start.1 = ((bf16[4,64,1,640]{3,0,2,1:T(4,128)(2,1)}), bf16[4,64,1,640]{3,0,2,1:T(4,128)(2,1)S(1)}, u32[]{:S(2)}, u32[]{:S(2)}) async-start(bf16[4,64,1,640]{3,0,2,1:T(4,128)(2,1)} %copy.32), calls=%async_computation.1 | async-start | bytes 655360 | tf_op jit(solution)/shard_map/all_to_all | solution.py:55
  32.4 59.8 %copy-start.9 = (s32[256]{0:T(256)S(1)}, s32[256]{0:T(256)}, u32[]{:S(2)}) copy-start(s32[256]{0:T(256)} %param.18) | copy-start | bytes 3076
  56.1 29.5 %all-to-all-start.2 = ((bf16[4,64,1,640]{3,0,2,1:T(4,128)(2,1)}), bf16[4,64,1,640]{3,0,2,1:T(4,128)(2,1)S(1)}, u32[]{:S(2)}, u32[]{:S(2)}) async-start(bf16[4,64,1,640]{3,0,2,1:T(4,128)(2,1)} %copy.34), calls=%async_computation.2 | async-start | bytes 655360 | tf_op jit(solution)/shard_map/all_to_all | solution.py:56
  85.6 28.9 %all-to-all-start = ((bf16[4,64,1,640]{3,0,2,1:T(4,128)(2,1)}), bf16[4,64,1,640]{3,0,2,1:T(4,128)(2,1)S(1)}, u32[]{:S(2)}, u32[]{:S(2)}) async-start(bf16[4,64,1,640]{3,0,2,1:T(4,128)(2,1)} %copy.31), calls=%async_computation | async-start | bytes 655360 | tf_op jit(solution)/shard_map/all_to_all | solution.py:57
  92.1 205.6 %all-reduce.15.cloned.1.call-start = ((), (), s32[]{:S(2)}) async-start(), calls=%async_computation.6 | async-start | bytes 1310720 | tf_op jit(solution)/shard_map/psum | solution.py:106
  217.2 10.9 %copy-start.3 = (bf16[2,640,320]{1,2,0:T(8,128)(2,1)S(1)}, bf16[2,640,320]{1,2,0:T(8,128)(2,1)}, u32[]{:S(2)}) copy-start(bf16[2,640,320]{1,2,0:T(8,128)(2,1)} %param.21) | copy-start | bytes 2457604
  228.1 1.3 copy-start.4
  230.7 347.1 %all-reduce.9.cloned.1.call-start = ((), (), s32[]{:S(2)}) async-start(), calls=%async_computation.3 | async-start | bytes 2621440
  300.6 460.8 %all-reduce.13.cloned.1.call-start = ((), (), s32[]{:S(2)}) async-start(), calls=%async_computation.5 | async-start | bytes 1310720 | tf_op jit(solution)/shard_map/psum | solution.py:106
  689.2 1.3 copy-start.5
  690.5 71.0 %copy-start.10 = (bf16[2,320,640]{2,1,0:T(8,128)(2,1)S(1)}, bf16[2,320,640]{2,1,0:T(8,128)(2,1)}, u32[]{:S(2)}) copy-start(bf16[2,320,640]{2,1,0:T(8,128)(2,1)} %param.23) | copy-start | bytes 2457604
  691.7 349.7 %all-reduce.11.cloned.1.call-start = ((), (), s32[]{:S(2)}) async-start(), calls=%async_computation.4 | async-start | bytes 2621440
Sparse Core Ops, SparseCore 0:
  230.8 66.8 all-reduce.14
  301.1 276.7 all-reduce.8
  691.8 69.5 all-reduce.12
  764.6 276.7 all-reduce.10
where the time goes:
time: 1050 us
  waiting for transfers between devices  754 us (72%)
  blocking collectives  219 us (21%)
  starting transfers between devices  32.1 us (3%)
  matrix products  14.3 us (1%)
  between operations  14.1 us (1%)
  local copies, waits for them, and re-layouts  10.9 us (1%)
    unnamed x6, waiting for transfers between devices  552 us
    all_gather x2, blocking collectives, per_device(): nodes = lax.all_gather(own_rows, 'gx', axis=0, tiled=True)  199 us
    psum x2, waiting for transfers between devices, per_device(): lax.psum(up_part.astype(jnp.bfloat16), 'ta').astype(jnp.float32)  137 us
    all_to_all x1, waiting for transfers between devices, per_device(): lax.all_to_all(sorted_queries, 'gx', split_axis=1, concat_axis=0, tiled=T...  22.7 us
    all_to_all x1, waiting for transfers between devices, per_device(): lax.all_to_all(sorted_keys, 'gx', split_axis=1, concat_axis=0, tiled=True)  21.6 us
  transfers between devices with their start and end apart: 7, of which 7 were waited for; matrix products, arithmetic and copies ran while one was open for 0% of the time, Pallas kernels for 0%

commit v1 on v0

--- a/solution.py
+++ b/solution.py
@@ -10,6 +10,12 @@
 NODE_STEPS = 8
 ROUNDS = 2
 ETYPES = 3
+
+
+def track_spots(inp, dim_no=0):
+    current_value = jnp.stack([inp for _ in range(jax.lax.axis_size("gx"))])
+    f_now = jax.lax.all_to_all(current_value, "gx", 0, 0)
+    return jnp.concatenate(f_now, dim_no)
 
 
 def settle_rows(nodes, hidden, down_local, row_begin, rows_dev):
@@ -111,7 +117,7 @@
             own_rows = settle_rows(nodes, hidden, down_local, row_begin, rows_dev)
         else:
             own_rows = settle_rows(nodes, hidden, down_local, row_begin, rows_dev)
-            nodes = lax.all_gather(own_rows, "gx", axis=0, tiled=True)
+            nodes = track_spots(own_rows)
     return own_rows
 
 

time: 1050 us -> 987 us (0.940)
  blocking collectives: 219 us -> 120 us
  waiting for transfers between devices: 754 us -> 779 us
    all_gather x2 -> x1, blocking collectives: 199 us -> 99.8 us  [per_device(): nodes = lax.all_gather(own_rows, 'gx', axis=0, tiled=True)]
    all_to_all x0 -> x1, waiting for transfers between devices: none -> 26.7 us  [track_spots(): f_now = jax.lax.all_to_all(current_value, 'gx', 0, 0)]
  transfers between devices with their start and end apart: 7 -> 8, of which waited for: 7 -> 8; matrix products, arithmetic and copies ran while one was open for 0% -> 0% of each run, Pallas kernels for 0% -> 0%
where the time goes in v1:
time: 987 us
  waiting for transfers between devices  779 us (79%)
  blocking collectives  120 us (12%)
  starting transfers between devices  41.3 us (4%)
  matrix products  15.5 us (2%)
  between operations  14.1 us (1%)
  local copies, waits for them, and re-layouts  11.8 us (1%)
    unnamed x6, waiting for transfers between devices  553 us
    psum x2, waiting for transfers between devices, per_device(): lax.psum(up_part.astype(jnp.bfloat16), 'ta').astype(jnp.float32)  135 us
    all_gather x1, blocking collectives, per_device(): nodes = lax.all_gather(own_rows, 'gx', axis=0, tiled=True)  99.8 us
    all_to_all x1, waiting for transfers between devices, track_spots(): f_now = jax.lax.all_to_all(current_value, 'gx', 0, 0)  26.7 us
    all_to_all x1, waiting for transfers between devices, per_device(): lax.all_to_all(sorted_queries, 'gx', split_axis=1, concat_axis=0, tiled=T...  22.7 us
    all_to_all x1, waiting for transfers between devices, per_device(): lax.all_to_all(sorted_keys, 'gx', split_axis=1, concat_axis=0, tiled=True)  21.6 us
    all_to_all x1, waiting for transfers between devices, per_device(): lax.all_to_all(sorted_values, 'gx', split_axis=1, concat_axis=0, tiled=True)  20.9 us
    psum x2, blocking collectives, per_device(): squares = lax.psum(jnp.sum(pre_norm * pre_norm, axis=-1), 'ta')  20.1 us
  transfers between devices with their start and end apart: 8, of which 8 were waited for; matrix products, arithmetic and copies ran while one was open for 0% of the time, Pallas kernels for 0%

profile of v1, /device:TPU:2, one launch (start us, length us, event | category | flops | bytes accessed | tf_op | source)
XLA Modules:
  0.0 986.6 jit_solution(6853408950278894890)
XLA Ops:
  6.5 0.7 compare_and_fusion
  7.3 0.2 copy-done
  7.5 1.6 gather_fusion
  9.1 1.6 gather_fusion.1
  10.8 1.6 gather_fusion.2
  12.4 0.2 select_bitcast_fusion.1
  12.6 1.0 copy.47
  13.6 18.9 %all-to-all-start.1 = ((bf16[4,64,1,640]{3,0,2,1:T(4,128)(2,1)}), bf16[4,64,1,640]{3,0,2,1:T(4,128)(2,1)S(1)}, u32[]{:S(2)}, u32[]{:S(2)}) async-start(bf16[4,64,1,640]{3,0,2,1:T(4,128)(2,1)} %copy.47), calls=%async_computation.1 | async-start | bytes 655360 | tf_op jit(solution)/shard_map/all_to_all | solution.py:61
  32.4 1.0 copy.49
  33.4 22.7 %all-to-all-done.1 = bf16[4,64,1,640]{3,0,2,1:T(4,128)(2,1)S(1)} async-done(((bf16[4,64,1,640]{3,0,2,1:T(4,128)(2,1)}), bf16[4,64,1,640]{3,0,2,1:T(4,128)(2,1)S(1)}, u32[]{:S(2)}, u32[]{:S(2)}) %all-to-all-start.1) | async-done | bytes 327712 | tf_op jit(solution)/shard_map/all_to_all | solution.py:61
  56.1 6.5 all-to-all-start.2
  62.6 1.0 copy.46
  64.0 21.6 %all-to-all-done.2 = bf16[4,64,1,640]{3,0,2,1:T(4,128)(2,1)S(1)} async-done(((bf16[4,64,1,640]{3,0,2,1:T(4,128)(2,1)}), bf16[4,64,1,640]{3,0,2,1:T(4,128)(2,1)S(1)}, u32[]{:S(2)}, u32[]{:S(2)}) %all-to-all-start.2) | async-done | bytes 327712 | tf_op jit(solution)/shard_map/all_to_all | solution.py:62
  85.6 6.6 all-to-all-start
  92.2 0.2 fusion.5
  92.5 0.1 reshape.182
  92.7 0.1 reshape.185
  92.9 0.5 fusion.70
  93.3 0.3 fusion.4
  93.6 20.9 %all-to-all-done = bf16[4,64,1,640]{3,0,2,1:T(4,128)(2,1)S(1)} async-done(((bf16[4,64,1,640]{3,0,2,1:T(4,128)(2,1)}), bf16[4,64,1,640]{3,0,2,1:T(4,128)(2,1)S(1)}, u32[]{:S(2)}, u32[]{:S(2)}) %all-to-all-start) | async-done | bytes 327712 | tf_op jit(solution)/shard_map/all_to_all | solution.py:63
  114.5 0.1 reshape.180
  114.7 1.4 convolution_bitcast_fusion
  116.0 0.2 copy.52
  116.4 99.8 %all_gather.3 = bf16[512,640]{1,0:T(8,128)(2,1)S(1)} all-gather(bf16[8,640]{1,0:T(8,128)(2,1)S(1)} %multiply_convert_fusion.2), channel_id=1, replica_groups=mesh['gx'=64,'ta'=8] {'gx'}, dimensions={0}, use_global_device_ids=true | all-gather | bytes 665600 | tf_op jit(solution)/shard_map/all_gather | solution.py:86
  216.2 0.3 reshape.187
  216.5 0.7 multiply_reduce_fusion.1
  217.2 0.9 multiply_reduce_fusion.3
  218.1 10.1 %psum.42 = f32[512]{0:T(512)S(1)} all-reduce(f32[512]{0:T(512)S(1)} %get-tuple-element.12), channel_id=1, replica_groups=mesh['gx'=64,'ta'=8] {'ta'}, use_global_device_ids=true, to_apply=%region_6.8 | all-reduce | flops 512 | bytes 4096 | tf_op jit(solution)/shard_map/psum | solution.py:105
  228.3 2.3 convolution_convert_fusion.3
  230.6 1.3 convolution_convert_fusion.2
  231.9 67.0 %all-reduce.15.cloned.1.call-done = (bf16[512,320]{0,1:T(8,128)(2,1)}, bf16[512,320]{0,1:T(8,128)(2,1)}) async-done(((bf16[512,320]{0,1:T(8,128)(2,1)}, bf16[512,320]{0,1:T(8,128)(2,1)}), (bf16[512,320]{0,1:T(8,128)(2,1)}, bf16[512,320]{0,1:T(8,128)(2,1)})) %all-reduce.15.cloned.1.call-update) | async-done | bytes 655376 | tf_op jit(solution)/shard_map/psum | solution.py:112
  298.9 2.9 fusion.26
  301.8 1.3 dynamic-slice
  303.7 275.3 %all-reduce.9.cloned.1.call-done = f32[512,640]{1,0:T(8,128)} async-done(((f32[512,640]{1,0:T(8,128)}), f32[512,640]{1,0:T(8,128)}) %all-reduce.9.cloned.1.call-update) | async-done | bytes 1310736
  579.0 0.7 fusion.54
  579.7 0.9 stack.2
  580.6 9.2 all-to-all-start.3
  589.9 26.7 %all-to-all-done.3 = bf16[64,8,640]{2,1,0:T(8,128)(2,1)S(1)} async-done(((bf16[64,8,640]{2,1,0:T(8,128)(2,1)}), bf16[64,8,640]{2,1,0:T(8,128)(2,1)S(1)}, u32[]{:S(2)}, u32[]{:S(2)}) %all-to-all-start.3) | async-done | bytes 655392 | tf_op jit(solution)/shard_map/all_to_all | solution.py:17
  616.6 0.7 multiply_reduce_fusion
  617.3 0.3 multiply_reduce_fusion.2
  617.8 10.0 %psum.45 = f32[512]{0:T(512)S(1)} all-reduce(f32[512]{0:T(512)S(1)} %reduce_sum.75), channel_id=1, replica_groups=mesh['gx'=64,'ta'=8] {'ta'}, use_global_device_ids=true, to_apply=%region_12.14 | all-reduce | flops 512 | bytes 4096 | tf_op jit(solution)/shard_map/psum | solution.py:105
  628.0 0.3 multiply_convert_fusion
  628.3 1.3 convolution_convert_fusion
  629.6 1.3 convolution_convert_fusion.1
  631.0 67.7 %all-reduce.13.cloned.1.call-done = (bf16[512,320]{0,1:T(8,128)(2,1)}, bf16[512,320]{0,1:T(8,128)(2,1)}) async-done(((bf16[512,320]{0,1:T(8,128)(2,1)}, bf16[512,320]{0,1:T(8,128)(2,1)}), (bf16[512,320]{0,1:T(8,128)(2,1)}, bf16[512,320]{0,1:T(8,128)(2,1)})) %all-reduce.13.cloned.1.call-update) | async-done | bytes 655376 | tf_op jit(solution)/shard_map/psum | solution.py:112
  698.7 2.8 fusion.22
  701.5 277.2 %all-reduce.11.cloned.1.call-done = f32[512,640]{1,0:T(8,128)} async-done(((f32[512,640]{1,0:T(8,128)}), f32[512,640]{1,0:T(8,128)}) %all-reduce.11.cloned.1.call-update) | async-done | bytes 1310736
  978.7 1.3 fusion.53
  (52 shorter events, 1.2 us)
Async XLA Ops:
  6.5 1.0 copy-start
  7.5 1.6 copy-start.1
  9.1 1.6 copy-start.2
  13.5 50.0 %copy-start.5 = (f32[2,3,640]{2,0,1:T(2,128)S(1)}, f32[2,3,640]{2,0,1:T(2,128)}, u32[]{:S(2)}) copy-start(f32[2,3,640]{2,0,1:T(2,128)} %param.19) | copy-start | bytes 46084
  13.5 50.1 %copy-start.7 = (s32[256,2]{0,1:T(2,128)S(1)}, s32[256,2]{0,1:T(2,128)}, u32[]{:S(2)}) copy-start(s32[256,2]{0,1:T(2,128)} %param.17) | copy-start | bytes 6148
  13.5 50.4 %copy-start.6 = (f32[2,640]{1,0:T(2,128)S(1)}, f32[2,640]{1,0:T(2,128)}, u32[]{:S(2)}) copy-start(f32[2,640]{1,0:T(2,128)} %param.20) | copy-start | bytes 15364
  13.6 42.6 %all-to-all-start.1 = ((bf16[4,64,1,640]{3,0,2,1:T(4,128)(2,1)}), bf16[4,64,1,640]{3,0,2,1:T(4,128)(2,1)S(1)}, u32[]{:S(2)}, u32[]{:S(2)}) async-start(bf16[4,64,1,640]{3,0,2,1:T(4,128)(2,1)} %copy.47), calls=%async_computation.1 | async-start | bytes 655360 | tf_op jit(solution)/shard_map/all_to_all | solution.py:61
  32.4 59.8 %copy-start.8 = (s32[256]{0:T(256)S(1)}, s32[256]{0:T(256)}, u32[]{:S(2)}) copy-start(s32[256]{0:T(256)} %param.18) | copy-start | bytes 3076
  56.1 29.5 %all-to-all-start.2 = ((bf16[4,64,1,640]{3,0,2,1:T(4,128)(2,1)}), bf16[4,64,1,640]{3,0,2,1:T(4,128)(2,1)S(1)}, u32[]{:S(2)}, u32[]{:S(2)}) async-start(bf16[4,64,1,640]{3,0,2,1:T(4,128)(2,1)} %copy.49), calls=%async_computation.2 | async-start | bytes 655360 | tf_op jit(solution)/shard_map/all_to_all | solution.py:62
  85.6 28.9 %all-to-all-start = ((bf16[4,64,1,640]{3,0,2,1:T(4,128)(2,1)}), bf16[4,64,1,640]{3,0,2,1:T(4,128)(2,1)S(1)}, u32[]{:S(2)}, u32[]{:S(2)}) async-start(bf16[4,64,1,640]{3,0,2,1:T(4,128)(2,1)} %copy.46), calls=%async_computation | async-start | bytes 655360 | tf_op jit(solution)/shard_map/all_to_all | solution.py:63
  92.1 206.7 %all-reduce.15.cloned.1.call-start = ((), (), s32[]{:S(2)}) async-start(), calls=%async_computation.7 | async-start | bytes 1310720 | tf_op jit(solution)/shard_map/psum | solution.py:112
  218.1 12.4 %copy-start.3 = (bf16[2,640,320]{1,2,0:T(8,128)(2,1)S(1)}, bf16[2,640,320]{1,2,0:T(8,128)(2,1)}, u32[]{:S(2)}) copy-start(bf16[2,640,320]{1,2,0:T(8,128)(2,1)} %param.22) | copy-start | bytes 2457604
  231.8 347.1 %all-reduce.9.cloned.1.call-start = ((), (), s32[]{:S(2)}) async-start(), calls=%async_computation.4 | async-start | bytes 2621440
  580.6 36.0 %all-to-all-start.3 = ((bf16[64,8,640]{2,1,0:T(8,128)(2,1)}), bf16[64,8,640]{2,1,0:T(8,128)(2,1)S(1)}, u32[]{:S(2)}, u32[]{:S(2)}) async-start(bf16[64,8,640]{2,1,0:T(8,128)(2,1)} %stack.2), calls=%async_computation.3 | async-start | bytes 1310720 | tf_op jit(solution)/shard_map/all_to_all | solution.py:17
  589.8 108.9 %all-reduce.13.cloned.1.call-start = ((), (), s32[]{:S(2)}) async-start(), calls=%async_computation.6 | async-start | bytes 1310720 | tf_op jit(solution)/shard_map/psum | solution.py:112
  628.3 1.3 copy-start.4
  629.6 69.1 %copy-start.9 = (bf16[2,320,640]{2,1,0:T(8,128)(2,1)S(1)}, bf16[2,320,640]{2,1,0:T(8,128)(2,1)}, u32[]{:S(2)}) copy-start(bf16[2,320,640]{2,1,0:T(8,128)(2,1)} %param.23) | copy-start | bytes 2457604
  631.0 347.7 %all-reduce.11.cloned.1.call-start = ((), (), s32[]{:S(2)}) async-start(), calls=%async_computation.5 | async-start | bytes 2621440
Sparse Core Ops, SparseCore 0:
  232.0 66.8 all-reduce.14
  302.2 276.7 all-reduce.8
  631.1 67.5 all-reduce.12
  701.9 276.7 all-reduce.10
